TPU v7x, 128 devices: a whole 4x4x4 slice. The times are simulated.
128 devices in a mesh: seq: 16 (over y, x_hi, core), head: 8 (over z, x_lo).
Axes of the slice: x: 4 (x_hi: 2, x_lo: 2; x = x_hi * 2 + x_lo), y: 4, z: 4, core: 2. Of those that a mesh axis runs over, the one named last changes fastest.
Arguments:
- queries: bfloat16 [2048, 8192], P('seq', 'head'), may hold values from -24 to 24
- key_rows: bfloat16 [2048, 1024], P('seq', 'head'), may hold values from -6 to 6
- value_rows: bfloat16 [2048, 1024], P('seq', 'head'), may hold values from -6 to 6
- out_weight: bfloat16 [8192, 8192], P('head'), may hold values from -0.5 to 0.5
- residual: bfloat16 [2048, 8192], P('seq', 'head'), may hold values from -54 to 54
- norm_gain: float32 [8192], replicated, may hold values from 0.1 to 1.9
- gate_weight: bfloat16 [8192, 28672], P(None, ('seq', 'head')), may hold values from -0.0625 to 0.0625
- up_weight: bfloat16 [8192, 28672], P(None, ('seq', 'head')), may hold values from -0.0625 to 0.0625
Outputs:
- edit_keys: bfloat16 [2048, 28672], P(None, ('seq', 'head'))
- hidden_state: bfloat16 [2048, 8192], P('seq', 'head')
All inputs are finite; a program needn't handle non-finite values.
Results may differ from a plain program's by a relative error of at most 0.019.
Values may be sent and summed in bfloat16 or wider, within the bound.
No kernel may reach another device: no remote copies, remote signals or barrier semaphores. Data moves between devices by JAX's collectives and lax.ppermute only.
A program may use at most 128 MiB of HBM per device.

v0:
```python
import jax
import jax.numpy as jnp
from jax import lax
from jax.sharding import PartitionSpec as P

HD = 128
very_low = -1e30


def attend_block(carry_state, rows, places, key_piece, value_piece, key_places):
    maxima, totals, accumulated = carry_state
    scores = jnp.einsum(
        "rkgd,nkd->kgrn", rows, key_piece, preferred_element_type=jnp.float32
    ) / jnp.sqrt(jnp.float32(HD))
    visible = places[:, None] >= key_places[None, :]
    scores = jnp.where(visible, scores, jnp.float32(very_low))
    new_maxima = jnp.maximum(maxima, jnp.max(scores, axis=-1))
    weights = jnp.exp(scores - new_maxima[..., None])
    totals = jnp.sum(weights, axis=-1)
    products = jnp.einsum(
        "kgrn,nkd->kgrd", weights, value_piece.astype(jnp.float32), precision=lax.Precision.HIGHEST
    )
    accumulated = products
    return (new_maxima, totals, accumulated)


def maybe_attend(current, rows, places, key_piece, value_piece, key_places, first_row):

    def compute(carry_state):
        return attend_block(carry_state, rows, places, key_piece, value_piece, key_places)

    def unchanged(carry_state):
        return carry_state

    return lax.cond(first_row <= places[-1], compute, unchanged, current)


def finish_rows(carry_state, row_count, width):
    maxima, totals, accumulated = carry_state
    result = accumulated / totals[..., None]
    return result.transpose(2, 0, 1, 3).reshape(row_count, width).astype(jnp.bfloat16)


def per_device(
    queries, key_rows, value_rows, out_weight, residual, norm_gain, gate_weight, up_weight
):
    tok_count = queries.shape[0]
    seq_index = lax.axis_index("seq")
    head_index = lax.axis_index("head")
    kv_local = key_rows.shape[1] // HD
    q_local = queries.shape[1] // HD
    group_size = q_local // kv_local
    own_first = seq_index * tok_count
    query_sets = ((queries, own_first + jnp.arange(tok_count, dtype=jnp.int32)),)
    shaped = tuple(
        (
            (rows.reshape(rows.shape[0], kv_local, group_size, HD), places)
            for rows, places in query_sets
        )
    )
    initial = tuple(
        (
            (
                jnp.full((kv_local, group_size, rows.shape[0]), very_low, jnp.float32),
                jnp.zeros((kv_local, group_size, rows.shape[0]), jnp.float32),
                jnp.zeros((kv_local, group_size, rows.shape[0], HD), jnp.float32),
            )
            for rows, places in shaped
        )
    )
    first_row = jnp.int32(0)
    key_piece = lax.all_gather(key_rows, "seq", axis=0, tiled=True).reshape(-1, kv_local, HD)
    value_piece = lax.all_gather(value_rows, "seq", axis=0, tiled=True).reshape(-1, kv_local, HD)
    key_places = jnp.arange(key_piece.shape[0], dtype=jnp.int32)
    updated = []
    for (fold_rows, fold_places), current in zip(shaped, initial):
        updated.append(
            maybe_attend(
                current, fold_rows, fold_places, key_piece, value_piece, key_places, first_row
            )
        )
    final_states = tuple(updated)
    finished = [
        finish_rows(state, rows.shape[0], q_local * HD)
        for state, (rows, places) in zip(final_states, shaped)
    ]
    attended = finished[0]
    projected = jnp.dot(attended, out_weight, preferred_element_type=jnp.float32)
    width_total = out_weight.shape[1]
    width_local = residual.shape[1]
    column_first = head_index * width_local
    shared_sum = lax.psum_scatter(
        projected.astype(jnp.bfloat16), "head", scatter_dimension=1, tiled=True
    ).astype(jnp.float32)
    hidden_state = (residual.astype(jnp.float32) + shared_sum).astype(jnp.bfloat16)
    widened = hidden_state.astype(jnp.float32)
    square_sum = lax.psum(jnp.sum(widened * widened, axis=-1, keepdims=True), "head")
    gain_local = lax.dynamic_slice_in_dim(norm_gain, column_first, width_local, 0)
    normed_local = (
        widened * lax.rsqrt(square_sum / width_total + 1e-05) * gain_local[None, :]
    ).astype(jnp.bfloat16)
    normed_full = lax.all_gather(normed_local, "head", axis=1, tiled=True)
    shard_rows = lax.all_gather(normed_full, "seq", axis=0, tiled=True)
    gate_sums = jnp.dot(shard_rows, gate_weight, preferred_element_type=jnp.float32)
    up_sums = jnp.dot(shard_rows, up_weight, preferred_element_type=jnp.float32)
    edit_keys = (jax.nn.silu(gate_sums) * up_sums).astype(jnp.bfloat16)
    return (edit_keys, hidden_state)


def solution(mesh):
    return jax.shard_map(
        per_device,
        mesh=mesh,
        in_specs=(
            P("seq", "head"),
            P("seq", "head"),
            P("seq", "head"),
            P("head", None),
            P("seq", "head"),
            P(),
            P(None, ("seq", "head")),
            P(None, ("seq", "head")),
        ),
        out_specs=(P(None, ("seq", "head")), P("seq", "head")),
        check_vma=False,
    )
```

profile of v0, /device:TPU:1, one launch (start us, length us, event | category | flops | bytes accessed | tf_op | source)
XLA Modules:
  0.0 428.1 jit_solution(579743415194872696)
XLA Ops:
  7.2 0.0 reduce-scatter.2.cloned.1.call-start
  7.2 0.6 slice.3
  8.5 28.2 %all_gather.12 = bf16[2048,128]{1,0:T(8,128)(2,1)S(1)} all-gather(bf16[128,128]{1,0:T(8,128)(2,1)} %param.11), channel_id=1, replica_groups=mesh['seq'=16,'head'=8] {'seq'}, dimensions={0}, use_global_device_ids=true | all-gather | bytes 557056 | tf_op jit(solution)/shard_map/all_gather | solution.py:72
  36.7 21.8 %all_gather.13 = bf16[2048,128]{1,0:T(8,128)(2,1)S(1)} all-gather(bf16[128,128]{1,0:T(8,128)(2,1)} %param.12), channel_id=1, replica_groups=mesh['seq'=16,'head'=8] {'seq'}, dimensions={0}, use_global_device_ids=true | all-gather | bytes 557056 | tf_op jit(solution)/shard_map/all_gather | solution.py:73
  58.5 8.9 %conditional.1 = (f32[1,8,128]{2,1,0:T(8,128)S(1)}, f32[1,8,128,128]{2,3,1,0:T(8,128)S(1)}) conditional(s32[]{:T(128)} %bitcast.7, () %tuple.16, (s32[128]{0:T(128)S(1)}, s32[2048]{0:T(1024)S(1)}, bf16[128,1024]{1,0:T(8,128)(2,1)}, bf16[2048,128]{1,0:T(8,128)(2,1)S(1)}, bf16[2048,128]{1,0:T(8,128)(2,1)S(1)}) %tuple.17), branch_computations={%region_0.0_spmd, %region_1.4_spmd} | conditional | flops 3779329024 | bytes 28082704 | solution.py:35
  58.5 0.3 broadcast_compare_fusion
  58.8 2.3 fusion.3
  61.1 4.6 %fusion.8 = f32[1,8,128,128]{2,3,1,0:T(8,128)S(1)} fusion(f32[2048,128,8]{1,0,2:T(8,128)S(1)} %get-tuple-element.30, f32[8,128]{1,0:T(8,128)S(1)} %broadcast_maximum_fusion, pred[128,2048]{0,1:T(8,128)(4,1)S(1)} %broadcast_compare_fusion, bf16[2048,128]{1,0:T(8,128)(2,1)S(1)} %get-tuple-element.17), kind=kOutput, calls=%fused_computation.10 | convolution fusion | flops 3227516928 | bytes 9703424 | tf_op jit(solution)/shard_map/cond/branch_1_fun/kgrn,nkd->kgrd/dot_general | solution.py:20
  65.7 1.7 fusion.2
  67.4 0.1 divide_convert_fusion
  67.5 0.0 copy-start.1
  67.5 9.6 %convolution_convert_fusion = bf16[128,8192]{1,0:T(8,128)(2,1)} fusion(bf16[128,1024]{0,1:T(8,128)(2,1)S(1)} %bitcast.53, bf16[1024,8192]{1,0:T(8,128)(2,1)} %param.13), kind=kOutput, calls=%fused_computation.20 | convolution fusion | flops 2148532224 | bytes 19136512 | tf_op jit(solution)/shard_map/dot_general | solution.py:88
  77.1 0.0 reduce-scatter.2.cloned.1.call-update
  77.1 0.0 all-gather.3.cloned.1.call-start
  77.2 0.7 dynamic_slice.3
  77.9 51.4 %reduce-scatter.2.cloned.1.call-done = bf16[128,1024]{1,0:T(8,128)(2,1)} async-done(((bf16[128,8192]{1,0:T(8,128)(2,1)}), bf16[128,1024]{1,0:T(8,128)(2,1)}) %reduce-scatter.2.cloned.1.call-update) | async-done | bytes 262160 | tf_op jit(solution)/shard_map/reduce_scatter | solution.py:92
  129.3 0.0 copy-done.1
  129.3 1.1 fusion.19
  130.4 0.0 copy-start
  130.4 13.3 %psum.7 = f32[128,1]{0,1:T(1,128)S(1)} all-reduce(f32[128,1]{0,1:T(1,128)S(1)} %bitcast.56), channel_id=1, replica_groups=mesh['seq'=16,'head'=8] {'head'}, use_global_device_ids=true, to_apply=%region_6.7 | all-reduce | flops 128 | bytes 1024 | tf_op jit(solution)/shard_map/psum | solution.py:97
  143.7 0.8 fusion.21
  144.6 0.0 all-gather.3.cloned.1.call-update
  144.6 0.2 all-gather.5.cloned.1.call-start
  144.8 54.0 %all-gather.3.cloned.1.call-done = bf16[128,8192]{1,0:T(8,128)(2,1)} async-done(((bf16[128,1024]{1,0:T(8,128)(2,1)}), bf16[128,8192]{1,0:T(8,128)(2,1)}) %all-gather.3.cloned.1.call-update) | async-done | bytes 2097168 | tf_op jit(solution)/shard_map/all_gather | solution.py:102
  198.9 0.0 all-gather.5.cloned.1.call-update
  198.9 188.1 %all-gather.5.cloned.1.call-done = bf16[2048,8192]{1,0:T(8,128)(2,1)} async-done(((bf16[128,8192]{1,0:T(8,128)(2,1)}), bf16[2048,8192]{1,0:T(8,128)(2,1)}) %all-gather.5.cloned.1.call-update) | async-done | bytes 33554448 | tf_op jit(solution)/shard_map/all_gather | solution.py:103
  386.9 0.0 copy-start.2
  387.0 17.3 %fusion.22 = f32[2048,224]{0,1:T(8,128)S(1)} fusion(bf16[2048,8192]{1,0:T(8,128)(2,1)} %all-gather.5.cloned.1.call-done, bf16[8192,224]{0,1:T(8,128)(2,1)} %param.16), kind=kOutput, calls=%fused_computation.32 | convolution fusion | flops 7516192768 | bytes 39059456 | tf_op jit(solution)/shard_map/dot_general | solution.py:104
  404.2 0.0 copy-done
  404.2 0.0 copy-done.2
  404.2 17.3 %fusion.18 = bf16[2048,224]{0,1:T(8,128)(2,1)} fusion(bf16[2048,8192]{1,0:T(8,128)(2,1)} %all-gather.5.cloned.1.call-done, bf16[8192,224]{0,1:T(8,128)(2,1)S(1)} %copy-done.2, f32[2048,224]{0,1:T(8,128)S(1)} %fusion.22), kind=kOutput, calls=%fused_computation.22 | convolution fusion | flops 7518945280 | bytes 39976960 | tf_op jit(solution)/shard_map/dot_general | solution.py:105
  (4 shorter events, 0.0 us)
Async XLA Ops:
  7.2 122.1 %reduce-scatter.2.cloned.1.call-start = ((), (), s32[]{:S(2)}) async-start(), calls=%async_computation.1 | async-start | bytes 2359296 | tf_op jit(solution)/shard_map/reduce_scatter | solution.py:92
  67.5 61.8 %copy-start.1 = (bf16[128,1024]{1,0:T(8,128)(2,1)S(1)}, bf16[128,1024]{1,0:T(8,128)(2,1)}, u32[]{:S(2)}) copy-start(bf16[128,1024]{1,0:T(8,128)(2,1)} %param.14) | copy-start | bytes 786436
  77.1 121.7 %all-gather.3.cloned.1.call-start = ((), (), s32[]{:S(2)}) async-start(), calls=%async_computation.2 | async-start | bytes 2359296 | tf_op jit(solution)/shard_map/all_gather | solution.py:102
  130.4 273.8 %copy-start = (bf16[128,1024]{1,0:T(8,128)(2,1)}, bf16[128,1024]{1,0:T(8,128)(2,1)S(1)}, u32[]{:S(2)}) copy-start(bf16[128,1024]{1,0:T(8,128)(2,1)S(1)} %get-tuple-element.28) | copy-start | bytes 786436
  144.6 242.4 %all-gather.5.cloned.1.call-start = ((), (), s32[]{:S(2)}) async-start(), calls=%async_computation.3 | async-start | bytes 35651584 | tf_op jit(solution)/shard_map/all_gather | solution.py:103
  386.9 17.3 %copy-start.2 = (bf16[8192,224]{0,1:T(8,128)(2,1)S(1)}, bf16[8192,224]{0,1:T(8,128)(2,1)}, u32[]{:S(2)}) copy-start(bf16[8192,224]{0,1:T(8,128)(2,1)} %param.17) | copy-start | bytes 11010052
Sparse Core Ops, SparseCore 0:
  77.3 51.9 reduce-scatter.1
  144.7 54.1 all-gather.2
  201.3 185.5 all-gather.4
where the time goes:
time: 428 us
  waiting for transfers between devices  294 us (69%)
  blocking collectives  63.3 us (15%)
  matrix products  51.1 us (12%)
  between operations  14.5 us (3%)
    all_gather x1, waiting for transfers between devices, per_device(): shard_rows = lax.all_gather(normed_full, 'seq', axis=0, tiled=True)  188 us
    all_gather x1, waiting for transfers between devices, per_device(): normed_full = lax.all_gather(normed_local, 'head', axis=1, tiled=True)  54 us
    reduce_scatter x1, waiting for transfers between devices, per_device(): lax.psum_scatter(projected.astype(jnp.bfloat16), 'head', scatter_dimensio...  51.4 us
    all_gather x1, blocking collectives, per_device(): lax.all_gather(key_rows, 'seq', axis=0, tiled=True)  28.2 us
    all_gather x1, blocking collectives, per_device(): lax.all_gather(value_rows, 'seq', axis=0, tiled=True)  21.8 us
    dot_general x1, matrix products, per_device(): up_sums = jnp.dot(shard_rows, up_weight, preferred_element_type=jnp.float32)  17.3 us
    dot_general x1, matrix products, per_device(): jnp.dot(shard_rows, gate_weight, preferred_element_type=jnp.float32)  17.3 us
    psum x1, blocking collectives, per_device(): lax.psum(jnp.sum(widened * widened, axis=-1, keepdims=True), 'head')  13.3 us
  transfers between devices with their start and end apart: 3, of which 3 were waited for; matrix products, arithmetic and copies ran while one was open for 0% of the time, Pallas kernels for 0%

commit v1 on v0

--- a/solution.py
+++ b/solution.py
@@ -5,6 +5,11 @@
 
 HD = 128
 very_low = -1e30
+
+
+def gather_over(shard, mesh_axis, along):
+    sent = jnp.stack([shard] * lax.axis_size(mesh_axis))
+    return jnp.concatenate(lax.all_to_all(sent, mesh_axis, 0, 0), axis=along)
 
 
 def attend_block(carry_state, rows, places, key_piece, value_piece, key_places):
@@ -70,7 +75,7 @@
     )
     first_row = jnp.int32(0)
     key_piece = lax.all_gather(key_rows, "seq", axis=0, tiled=True).reshape(-1, kv_local, HD)
-    value_piece = lax.all_gather(value_rows, "seq", axis=0, tiled=True).reshape(-1, kv_local, HD)
+    value_piece = gather_over(value_rows, "seq", 0).reshape(-1, kv_local, HD)
     key_places = jnp.arange(key_piece.shape[0], dtype=jnp.int32)
     updated = []
     for (fold_rows, fold_places), current in zip(shaped, initial):

time: 428 us -> 414 us (0.967)
  blocking collectives: 63.3 us -> 40.3 us
  starting transfers between devices: 0.3 us -> 8.56 us
    all_gather x1 -> x0, blocking collectives: 21.8 us -> none  [per_device(): lax.all_gather(value_rows, 'seq', axis=0, tiled=True)]
    all_to_all x0 -> x1, starting transfers between devices: none -> 8.44 us  [gather_over(): return jnp.concatenate(lax.all_to_all(sent, mesh_axis, 0, 0), axis=along)]
  transfers between devices with their start and end apart: 3 -> 4, of which waited for: 3 -> 3; matrix products, arithmetic and copies ran while one was open for 0% -> 0% of each run, Pallas kernels for 0% -> 0%
where the time goes in v1:
time: 414 us
  waiting for transfers between devices  292 us (71%)
  matrix products  51.1 us (12%)
  blocking collectives  40.3 us (10%)
  between operations  14.5 us (4%)
  starting transfers between devices  8.56 us (2%)
    all_gather x1, waiting for transfers between devices, per_device(): shard_rows = lax.all_gather(normed_full, 'seq', axis=0, tiled=True)  188 us
    all_gather x1, waiting for transfers between devices, per_device(): normed_full = lax.all_gather(normed_local, 'head', axis=1, tiled=True)  54.2 us
    reduce_scatter x1, waiting for transfers between devices, per_device(): lax.psum_scatter(projected.astype(jnp.bfloat16), 'head', scatter_dimensio...  49.8 us
    all_gather x1, blocking collectives, per_device(): lax.all_gather(key_rows, 'seq', axis=0, tiled=True)  26.8 us
    dot_general x1, matrix products, per_device(): up_sums = jnp.dot(shard_rows, up_weight, preferred_element_type=jnp.float32)  17.3 us
    dot_general x1, matrix products, per_device(): jnp.dot(shard_rows, gate_weight, preferred_element_type=jnp.float32)  17.2 us
    psum x1, blocking collectives, per_device(): lax.psum(jnp.sum(widened * widened, axis=-1, keepdims=True), 'head')  13.5 us
    dot_general x1, matrix products, per_device(): jnp.dot(attended, out_weight, preferred_element_type=jnp.float32)  9.62 us
  transfers between devices with their start and end apart: 4, of which 3 were waited for; matrix products, arithmetic and copies ran while one was open for 0% of the time, Pallas kernels for 0%

profile of v1, /device:TPU:1, one launch (start us, length us, event | category | flops | bytes accessed | tf_op | source)
XLA Modules:
  0.0 413.5 jit_solution(3300985366616468473)
XLA Ops:
  7.2 1.7 stack.2
  8.8 8.4 %all-to-all-start = ((bf16[16,128,128]{2,1,0:T(8,128)(2,1)}), bf16[16,128,128]{2,1,0:T(8,128)(2,1)S(1)}, u32[]{:S(2)}, u32[]{:S(2)}) async-start(bf16[16,128,128]{2,1,0:T(8,128)(2,1)} %stack.2), calls=%async_computation | async-start | bytes 1048576 | tf_op jit(solution)/shard_map/all_to_all | solution.py:12
  17.3 0.0 reduce-scatter.2.cloned.1.call-start
  17.3 0.6 slice.3
  18.5 26.8 %all_gather.9 = bf16[2048,128]{1,0:T(8,128)(2,1)S(1)} all-gather(bf16[128,128]{1,0:T(8,128)(2,1)} %param.11), channel_id=1, replica_groups=mesh['seq'=16,'head'=8] {'seq'}, dimensions={0}, use_global_device_ids=true | all-gather | bytes 557056 | tf_op jit(solution)/shard_map/all_gather | solution.py:77
  45.3 0.0 all-to-all-done
  45.3 9.0 %conditional.1 = (f32[1,8,128]{2,1,0:T(8,128)S(1)}, f32[1,8,128,128]{2,3,1,0:T(8,128)S(1)}) conditional(s32[]{:T(128)} %bitcast.8, () %tuple.16, (s32[128]{0:T(128)S(1)}, s32[2048]{0:T(1024)S(1)}, bf16[128,1024]{1,0:T(8,128)(2,1)}, bf16[2048,128]{1,0:T(8,128)(2,1)S(1)}, bf16[16,128,128]{2,1,0:T(8,128)(2,1)S(1)}) %tuple.17), branch_computations={%region_0.0_spmd, %region_1.4_spmd} | conditional | flops 3779329024 | bytes 28082704 | solution.py:40
  45.3 0.3 broadcast_compare_fusion
  45.7 2.3 fusion.3
  48.0 4.6 %fusion.8 = f32[1,8,128,128]{2,3,1,0:T(8,128)S(1)} fusion(bf16[2048,128,1]{1,0,2:T(8,128)(2,1)S(1)} %bitcast.55, f32[2048,128,8]{1,0,2:T(8,128)S(1)} %get-tuple-element.30, f32[8,128]{1,0:T(8,128)S(1)} %broadcast_maximum_fusion, pred[128,2048]{0,1:T(8,128)(4,1)S(1)} %broadcast_compare_fusion), kind=kOutput, calls=%fused_computation.10 | convolution fusion | flops 3227516928 | bytes 9703424 | tf_op jit(solution)/shard_map/cond/branch_1_fun/kgrn,nkd->kgrd/dot_general | solution.py:25
  52.6 1.7 fusion.2
  54.3 0.1 divide_convert_fusion
  54.3 0.0 copy-start.1
  54.3 9.6 %convolution_convert_fusion = bf16[128,8192]{1,0:T(8,128)(2,1)} fusion(bf16[128,1024]{0,1:T(8,128)(2,1)S(1)} %bitcast.54, bf16[1024,8192]{1,0:T(8,128)(2,1)} %param.13), kind=kOutput, calls=%fused_computation.19 | convolution fusion | flops 2148532224 | bytes 19136512 | tf_op jit(solution)/shard_map/dot_general | solution.py:93
  64.0 0.0 reduce-scatter.2.cloned.1.call-update
  64.0 0.0 all-gather.3.cloned.1.call-start
  64.1 0.7 dynamic_slice.3
  64.7 49.8 %reduce-scatter.2.cloned.1.call-done = bf16[128,1024]{1,0:T(8,128)(2,1)} async-done(((bf16[128,8192]{1,0:T(8,128)(2,1)}), bf16[128,1024]{1,0:T(8,128)(2,1)}) %reduce-scatter.2.cloned.1.call-update) | async-done | bytes 262160 | tf_op jit(solution)/shard_map/reduce_scatter | solution.py:97
  114.5 0.0 copy-done.1
  114.5 1.1 fusion.18
  115.6 0.0 copy-start
  115.6 13.5 %psum.7 = f32[128,1]{0,1:T(1,128)S(1)} all-reduce(f32[128,1]{0,1:T(1,128)S(1)} %bitcast.58), channel_id=1, replica_groups=mesh['seq'=16,'head'=8] {'head'}, use_global_device_ids=true, to_apply=%region_6.7 | all-reduce | flops 128 | bytes 1024 | tf_op jit(solution)/shard_map/psum | solution.py:102
  129.2 0.8 fusion.20
  130.0 0.0 all-gather.3.cloned.1.call-update
  130.0 0.0 all-gather.5.cloned.1.call-start
  130.1 54.2 %all-gather.3.cloned.1.call-done = bf16[128,8192]{1,0:T(8,128)(2,1)} async-done(((bf16[128,1024]{1,0:T(8,128)(2,1)}), bf16[128,8192]{1,0:T(8,128)(2,1)}) %all-gather.3.cloned.1.call-update) | async-done | bytes 2097168 | tf_op jit(solution)/shard_map/all_gather | solution.py:107
  184.3 0.0 all-gather.5.cloned.1.call-update
  184.3 188.1 %all-gather.5.cloned.1.call-done = bf16[2048,8192]{1,0:T(8,128)(2,1)} async-done(((bf16[128,8192]{1,0:T(8,128)(2,1)}), bf16[2048,8192]{1,0:T(8,128)(2,1)}) %all-gather.5.cloned.1.call-update) | async-done | bytes 33554448 | tf_op jit(solution)/shard_map/all_gather | solution.py:108
  372.4 17.2 %fusion.21 = f32[2048,224]{0,1:T(8,128)S(1)} fusion(bf16[2048,8192]{1,0:T(8,128)(2,1)} %all-gather.5.cloned.1.call-done, bf16[8192,224]{0,1:T(8,128)(2,1)} %param.16), kind=kOutput, calls=%fused_computation.31 | convolution fusion | flops 7516192768 | bytes 39059456 | tf_op jit(solution)/shard_map/dot_general | solution.py:109
  389.6 0.0 copy-done
  389.7 0.0 copy-done.2
  389.7 17.3 %fusion.17 = bf16[2048,224]{0,1:T(8,128)(2,1)} fusion(bf16[2048,8192]{1,0:T(8,128)(2,1)} %all-gather.5.cloned.1.call-done, bf16[8192,224]{0,1:T(8,128)(2,1)S(1)} %copy-done.2, f32[2048,224]{0,1:T(8,128)S(1)} %fusion.21), kind=kOutput, calls=%fused_computation.21 | convolution fusion | flops 7518945280 | bytes 39976960 | tf_op jit(solution)/shard_map/dot_general | solution.py:110
  (5 shorter events, 0.0 us)
Async XLA Ops:
  8.8 36.5 %all-to-all-start = ((bf16[16,128,128]{2,1,0:T(8,128)(2,1)}), bf16[16,128,128]{2,1,0:T(8,128)(2,1)S(1)}, u32[]{:S(2)}, u32[]{:S(2)}) async-start(bf16[16,128,128]{2,1,0:T(8,128)(2,1)} %stack.2), calls=%async_computation | async-start | bytes 1048576 | tf_op jit(solution)/shard_map/all_to_all | solution.py:12
  17.3 97.3 %reduce-scatter.2.cloned.1.call-start = ((), (), s32[]{:S(2)}) async-start(), calls=%async_computation.2 | async-start | bytes 2359296 | tf_op jit(solution)/shard_map/reduce_scatter | solution.py:97
  54.3 60.2 %copy-start.1 = (bf16[128,1024]{1,0:T(8,128)(2,1)S(1)}, bf16[128,1024]{1,0:T(8,128)(2,1)}, u32[]{:S(2)}) copy-start(bf16[128,1024]{1,0:T(8,128)(2,1)} %param.14) | copy-start | bytes 786436
  64.0 120.3 %all-gather.3.cloned.1.call-start = ((), (), s32[]{:S(2)}) async-start(), calls=%async_computation.3 | async-start | bytes 2359296 | tf_op jit(solution)/shard_map/all_gather | solution.py:107
  115.6 274.0 %copy-start = (bf16[128,1024]{1,0:T(8,128)(2,1)}, bf16[128,1024]{1,0:T(8,128)(2,1)S(1)}, u32[]{:S(2)}) copy-start(bf16[128,1024]{1,0:T(8,128)(2,1)S(1)} %get-tuple-element.28) | copy-start | bytes 786436
  130.0 242.4 %all-gather.5.cloned.1.call-start = ((), (), s32[]{:S(2)}) async-start(), calls=%async_computation.4 | async-start | bytes 35651584 | tf_op jit(solution)/shard_map/all_gather | solution.py:108
  372.4 17.3 %copy-start.2 = (bf16[8192,224]{0,1:T(8,128)(2,1)S(1)}, bf16[8192,224]{0,1:T(8,128)(2,1)}, u32[]{:S(2)}) copy-start(bf16[8192,224]{0,1:T(8,128)(2,1)} %param.17) | copy-start | bytes 11010052
Sparse Core Ops, SparseCore 0:
  64.1 50.3 reduce-scatter.1
  130.2 54.0 all-gather.2
  186.8 185.5 all-gather.4
